TPU v7x, 256 devices: a whole 4x4x8 slice. The times are simulated.
256 devices in a mesh: row: 8 (over z_hi, y), col: 32 (over z_lo, x, core).
Axes of the slice: x: 4, y: 4, z: 8 (z_hi: 2, z_lo: 4; z = z_hi * 4 + z_lo), core: 2. Of those that a mesh axis runs over, the one named last changes fastest.
Arguments:
- queries: bfloat16 [32768, 256], P(('row', 'col')), may hold values from -6 to 6
- keys: bfloat16 [32768, 256], P('col', 'row'), may hold values from -6 to 6
- values: bfloat16 [32768, 256], P('col', 'row'), may hold values from -0.59765625 to 0.59765625
- outputs: bfloat16 [32768, 256], P(('row', 'col')), may hold values from -0.59765625 to 0.59765625
- d_out: bfloat16 [32768, 256], P(('row', 'col')), may hold values from -6 to 6
- lse: float32 [2, 32768], P(None, ('row', 'col')), may hold values from 4 to 6
Outputs:
- d_queries: bfloat16 [32768, 256], P(('row', 'col'))
- d_keys: bfloat16 [32768, 256], P('col', 'row')
- d_values: bfloat16 [32768, 256], P('col', 'row')
All inputs are finite; a program needn't handle non-finite values.
Results may differ from a plain program's by a relative error of at most 0.0049.
Values may be sent and summed in bfloat16 or wider, within the bound.
No kernel may reach another device: no remote copies, remote signals or barrier semaphores. Data moves between devices by JAX's collectives and lax.ppermute only.
A program may use at most 64 MiB of HBM per device.

v0:
```python
import jax
import jax.numpy as jnp
from jax import lax
from jax.sharding import PartitionSpec as P


def block_size(row_total):
    block_rows = row_total
    while block_rows > 512 and block_rows % 2 == 0:
        block_rows = block_rows // 2
    return block_rows


def head_slice(matrix, head_index, head_dim):
    return matrix[:, head_index * head_dim : (head_index + 1) * head_dim]


def contract_rows(left, right):
    return lax.dot_general(
        left, right, (((0,), (0,)), ((), ())), preferred_element_type=jnp.float32
    )


def score_terms(query_head, grad_head, lse_row, delta_row, key_head, value_head, scaling):
    scores = jnp.dot(query_head, key_head.T, preferred_element_type=jnp.float32)
    probs = jnp.exp(scores * scaling - lse_row[:, None])
    probs_low = probs.astype(jnp.bfloat16)
    grad_probs = jnp.dot(grad_head, value_head.T, preferred_element_type=jnp.float32)
    grad_scores = (probs * (grad_probs - delta_row[:, None])).astype(jnp.bfloat16)
    return (probs_low, grad_scores)


def block_grads(query_rows, grad_rows, lse_rows, delta_rows, key_all, value_all, head_dim):
    head_total = lse_rows.shape[0]
    scaling = head_dim ** (-0.5)
    key_terms = []
    value_terms = []
    query_terms = []
    for head_index in range(head_total):
        query_head = head_slice(query_rows, head_index, head_dim)
        grad_head = head_slice(grad_rows, head_index, head_dim)
        key_head = head_slice(key_all, head_index, head_dim)
        value_head = head_slice(value_all, head_index, head_dim)
        probs_low, grad_scores = score_terms(
            query_head,
            grad_head,
            lse_rows[head_index],
            delta_rows[head_index],
            key_head,
            value_head,
            scaling,
        )
        value_terms.append(contract_rows(probs_low, grad_head))
        key_terms.append(contract_rows(grad_scores, query_head))
        query_terms.append(jnp.dot(grad_scores, key_head, preferred_element_type=jnp.float32))
    key_term = jnp.concatenate(key_terms, axis=1)
    value_term = jnp.concatenate(value_terms, axis=1)
    query_term = jnp.concatenate(query_terms, axis=1)
    return (key_term, value_term, query_term)


def split_blocks(query_all, grad_all, lse_all, delta_all):
    row_total, features = query_all.shape
    block_rows = block_size(row_total)
    steps_total = row_total // block_rows
    head_total = lse_all.shape[0]
    query_blocks = query_all.reshape(steps_total, block_rows, features)
    grad_blocks = grad_all.reshape(steps_total, block_rows, features)
    lse_blocks = lse_all.reshape(head_total, steps_total, block_rows).transpose(1, 0, 2)
    delta_blocks = delta_all.reshape(head_total, steps_total, block_rows).transpose(1, 0, 2)
    return (query_blocks, grad_blocks, lse_blocks, delta_blocks)


def query_pass(query_all, grad_all, lse_all, delta_all, key_all, value_all, head_dim):
    row_total, features = query_all.shape
    block_inputs = split_blocks(query_all, grad_all, lse_all, delta_all)
    empty_sums = jnp.zeros((key_all.shape[0], features), jnp.float32)

    def advance(running, inputs):
        key_sum, value_sum = running
        query_rows, grad_rows, lse_rows, delta_rows = inputs
        key_term, value_term, query_term = block_grads(
            query_rows, grad_rows, lse_rows, delta_rows, key_all, value_all, head_dim
        )
        return ((key_sum + key_term, value_sum + value_term), query_term)

    (key_sum, value_sum), query_terms = lax.scan(advance, (empty_sums, empty_sums), block_inputs)
    query_terms = query_terms.reshape(row_total, features)
    return (key_sum, value_sum, query_terms)


def head_delta(d_out, outputs, head_total, head_dim):
    product = d_out.astype(jnp.float32) * outputs.astype(jnp.float32)
    return jnp.sum(product.reshape(product.shape[0], head_total, head_dim), axis=2).T


def per_device(queries, keys, values, outputs, d_out, lse):
    head_total = lse.shape[0]
    head_dim = queries.shape[1] // head_total
    scaling = head_dim ** (-0.5)
    delta = head_delta(d_out, outputs, head_total, head_dim)
    key_all, value_all = (
        lax.all_gather(keys, "row", axis=1, tiled=True),
        lax.all_gather(values, "row", axis=1, tiled=True),
    )
    query_all, grad_all = (
        lax.all_gather(queries, "col", axis=0, tiled=True),
        lax.all_gather(d_out, "col", axis=0, tiled=True),
    )
    lse_all, delta_all = (
        lax.all_gather(lse, "col", axis=1, tiled=True),
        lax.all_gather(delta, "col", axis=1, tiled=True),
    )
    key_sum, value_sum, query_terms = query_pass(
        query_all, grad_all, lse_all, delta_all, key_all, value_all, head_dim
    )
    query_grad = lax.psum_scatter(query_terms, "col", scatter_dimension=0, tiled=True)
    key_grad, value_grad = (
        lax.psum_scatter(key_sum, "row", scatter_dimension=1, tiled=True),
        lax.psum_scatter(value_sum, "row", scatter_dimension=1, tiled=True),
    )
    d_queries = (query_grad * scaling).astype(jnp.bfloat16)
    d_keys = (key_grad * scaling).astype(jnp.bfloat16)
    d_values = value_grad.astype(jnp.bfloat16)
    return (d_queries, d_keys, d_values)


def solution(mesh):
    placed = (
        P(("row", "col"), None),
        P("col", "row"),
        P("col", "row"),
        P(("row", "col"), None),
        P(("row", "col"), None),
        P(None, ("row", "col")),
    )
    return jax.shard_map(
        per_device,
        mesh=mesh,
        in_specs=placed,
        out_specs=(P(("row", "col"), None), P("col", "row"), P("col", "row")),
        check_vma=False,
    )
```

profile of v0, /device:TPU:8, one launch (start us, length us, event | category | flops | bytes accessed | tf_op | source)
XLA Modules:
  0.0 613.3 jit_solution(17690217975706771563)
XLA Ops:
  9.7 47.4 %all_gather.19 = bf16[1024,256]{0,1:T(8,128)(2,1)S(1)} all-gather(bf16[1024,32]{0,1:T(8,128)(2,1)} %param.9), channel_id=1, replica_groups=mesh['row'=8,'col'=32] {'row'}, dimensions={1}, use_global_device_ids=true | all-gather | bytes 589824 | tf_op jit(solution)/shard_map/all_gather | solution.py:103
  57.4 45.8 %all_gather.22 = bf16[1024,256]{0,1:T(8,128)(2,1)S(1)} all-gather(bf16[1024,32]{0,1:T(8,128)(2,1)S(1)} %copy-done.1), channel_id=1, replica_groups=mesh['row'=8,'col'=32] {'row'}, dimensions={1}, use_global_device_ids=true | all-gather | bytes 589824 | tf_op jit(solution)/shard_map/all_gather | solution.py:104
  103.6 50.5 %all_gather.23 = f32[2,4096]{0,1:T(8,128)} all-gather(f32[2,128]{0,1:T(8,128)S(1)} %bitcast.55), channel_id=1, replica_groups=mesh['row'=8,'col'=32] {'col'}, dimensions={1}, use_global_device_ids=true | all-gather | bytes 33792 | tf_op jit(solution)/shard_map/all_gather | solution.py:112
  154.1 2.2 copy.19
  156.3 37.9 %all_gather.20 = f32[2,4096]{1,0:T(2,128)S(1)} all-gather(f32[2,128]{1,0:T(2,128)S(1)} %copy-done.2), channel_id=1, replica_groups=mesh['row'=8,'col'=32] {'col'}, dimensions={1}, use_global_device_ids=true | all-gather | bytes 33792 | tf_op jit(solution)/shard_map/all_gather | solution.py:111
  194.2 87.0 %while.15 = (s32[]{:T(128)}, f32[1024,256]{0,1:T(8,128)}, f32[1024,256]{0,1:T(8,128)S(1)}, f32[8,512,256]{2,1,0:T(8,128)}, bf16[8,512,256]{2,1,0:T(8,128)(2,1)},...) while((s32[]{:T(128)}, f32[1024,256]{0,1:T(8,128)}, ...), condition=%wide.region_2.3_spmd.clone, body=%wide.region_1.2_spmd.clone.sunk | while | flops 1352269824 | bytes 34631860 | solution.py:87
  195.2 1.0 dynamic-slice_bitcast_fusion.4
  201.2 1.8 maximum_add_fusion.3
  204.1 1.0 dynamic-slice_bitcast_fusion.5
  211.0 3.0 maximum_add_fusion.3
  216.0 1.0 dynamic-slice_bitcast_fusion.4
  222.0 3.0 maximum_add_fusion.3
  227.1 1.0 dynamic-slice_bitcast_fusion.4
  233.1 3.0 maximum_add_fusion.3
  244.1 3.0 maximum_add_fusion.3
  255.1 3.0 maximum_add_fusion.3
  266.2 3.0 maximum_add_fusion.3
  277.2 3.0 maximum_add_fusion.3
  283.4 85.4 %reduce-scatter.8.cloned.1.call-done = f32[1024,32]{0,1:T(8,128)} async-done(((f32[1024,256]{0,1:T(8,128)}), f32[1024,32]{0,1:T(8,128)}) %reduce-scatter.8.cloned.1.call-update) | async-done | bytes 131088 | tf_op jit(solution)/shard_map/reduce_scatter | solution.py:120
  368.8 1.5 convert_element_type.31
  370.3 85.5 %reduce-scatter.6.cloned.1.call-done = f32[1024,32]{0,1:T(8,128)} async-done(((f32[1024,256]{0,1:T(8,128)}), f32[1024,32]{0,1:T(8,128)}) %reduce-scatter.6.cloned.1.call-update) | async-done | bytes 131088 | tf_op jit(solution)/shard_map/reduce_scatter | solution.py:119
  455.9 1.5 multiply_convert_fusion.2
  457.4 147.8 %reduce-scatter.4.cloned.1.call-done = f32[128,256]{1,0:T(8,128)} async-done(((f32[4096,256]{1,0:T(8,128)}), f32[128,256]{1,0:T(8,128)}) %reduce-scatter.4.cloned.1.call-update) | async-done | bytes 131088 | tf_op jit(solution)/shard_map/reduce_scatter | solution.py:117
  605.2 1.5 multiply_convert_fusion.3
  (158 shorter events, 65.0 us)
Async XLA Ops:
  7.2 50.2 %copy-start.1 = (bf16[1024,32]{0,1:T(8,128)(2,1)S(1)}, bf16[1024,32]{0,1:T(8,128)(2,1)}, u32[]{:S(2)}) copy-start(bf16[1024,32]{0,1:T(8,128)(2,1)} %param.10) | copy-start | bytes 196612
  7.2 187.1 %all-gather.3.cloned.1.call-start = ((), (), s32[]{:S(2)}) async-start(), calls=%async_computation.3 | async-start | bytes 2162688 | tf_op jit(solution)/shard_map/all_gather | solution.py:107
  7.9 186.3 %all-gather.5.cloned.1.call-start = ((), (), s32[]{:S(2)}) async-start(), calls=%async_computation.4 | async-start | bytes 2162688 | tf_op jit(solution)/shard_map/all_gather | solution.py:108
  8.7 360.1 %reduce-scatter.8.cloned.1.call-start = ((), (), s32[]{:S(2)}) async-start(), calls=%async_computation.7 | async-start | bytes 1179648 | tf_op jit(solution)/shard_map/reduce_scatter | solution.py:120
  103.6 52.7 %copy-start.2 = (f32[2,128]{1,0:T(2,128)S(1)}, f32[2,128]{1,0:T(2,128)}, u32[]{:S(2)}) copy-start(f32[2,128]{1,0:T(2,128)} %param.13) | copy-start | bytes 3076
  281.2 1.0 copy-start
  282.2 173.6 %reduce-scatter.6.cloned.1.call-start = ((), (), s32[]{:S(2)}) async-start(), calls=%async_computation.6 | async-start | bytes 1179648 | tf_op jit(solution)/shard_map/reduce_scatter | solution.py:119
  282.8 322.4 %reduce-scatter.4.cloned.1.call-start = ((), (), s32[]{:S(2)}) async-start(), calls=%async_computation.5 | async-start | bytes 4325376 | tf_op jit(solution)/shard_map/reduce_scatter | solution.py:117
Sparse Core Ops, SparseCore 0:
  9.9 63.0 all-gather.2
  74.8 60.6 all-gather.4
  282.3 86.4 reduce-scatter.7
  373.1 82.7 reduce-scatter.5
  458.2 146.9 reduce-scatter.3
where the time goes:
time: 614 us; the launch traced here: 613 us
  waiting for transfers between devices  321 us (52%)
  blocking collectives  182 us (30%)
  matrix products  39.4 us (6%)
  other arithmetic  28.6 us (5%)
  local copies, waits for them, and re-layouts  27.7 us (5%)
  between operations  13.9 us (2%)
    reduce_scatter x1, waiting for transfers between devices, per_device(): lax.psum_scatter(query_terms, 'col', scatter_dimension=0, tiled=True)  148 us
    reduce_scatter x1, waiting for transfers between devices, per_device(): lax.psum_scatter(key_sum, 'row', scatter_dimension=1, tiled=True)  85.5 us
    reduce_scatter x1, waiting for transfers between devices, per_device(): lax.psum_scatter(value_sum, 'row', scatter_dimension=1, tiled=True)  85.4 us
    all_gather x1, blocking collectives, per_device(): lax.all_gather(delta, 'col', axis=1, tiled=True)  50.5 us
    all_gather x1, blocking collectives, per_device(): lax.all_gather(keys, 'row', axis=1, tiled=True)  47.4 us
    all_gather x1, blocking collectives, per_device(): lax.all_gather(values, 'row', axis=1, tiled=True)  45.8 us
    all_gather x1, blocking collectives, per_device(): lax.all_gather(lse, 'col', axis=1, tiled=True)  37.9 us
    add x8, other arithmetic, advance(): return ((key_sum + key_term, value_sum + value_term), query_term)  22.6 us
  transfers between devices with their start and end apart: 5, of which 3 were waited for; matrix products, arithmetic and copies ran while one was open for 1% of the time, Pallas kernels for 0%

commit v1 on v0

--- a/solution.py
+++ b/solution.py
@@ -101,7 +101,9 @@
     delta = head_delta(d_out, outputs, head_total, head_dim)
     key_all, value_all = (
         lax.all_gather(keys, "row", axis=1, tiled=True),
-        lax.all_gather(values, "row", axis=1, tiled=True),
+        jnp.concatenate(
+            lax.all_to_all(jnp.stack([values] * lax.axis_size("row")), "row", 0, 0), axis=1
+        ),
     )
     query_all, grad_all = (
         lax.all_gather(queries, "col", axis=0, tiled=True),

time: 614 us -> 584 us (0.951)
  blocking collectives: 182 us -> 137 us
  starting transfers between devices: 0.19 us -> 11.7 us
    all_gather x1 -> x0, blocking collectives: 45.8 us -> none  [per_device(): lax.all_gather(values, 'row', axis=1, tiled=True)]
    all_to_all x0 -> x1, starting transfers between devices: none -> 11.5 us  [per_device(): lax.all_to_all(jnp.stack([values] * lax.axis_size('row')), 'row', 0, 0)]
  transfers between devices with their start and end apart: 5 -> 6, of which waited for: 3 -> 3; matrix products, arithmetic and copies ran while one was open for 1% -> 1% of each run, Pallas kernels for 0% -> 0%
where the time goes in v1:
time: 584 us; the launch traced here: 582 us
  waiting for transfers between devices  322 us (55%)
  blocking collectives  137 us (23%)
  matrix products  39.4 us (7%)
  local copies, waits for them, and re-layouts  29.4 us (5%)
  other arithmetic  28.6 us (5%)
  between operations  13.8 us (2%)
  starting transfers between devices  11.7 us (2%)
    reduce_scatter x1, waiting for transfers between devices, per_device(): lax.psum_scatter(query_terms, 'col', scatter_dimension=0, tiled=True)  148 us
    reduce_scatter x1, waiting for transfers between devices, per_device(): lax.psum_scatter(value_sum, 'row', scatter_dimension=1, tiled=True)  86 us
    reduce_scatter x1, waiting for transfers between devices, per_device(): lax.psum_scatter(key_sum, 'row', scatter_dimension=1, tiled=True)  85.6 us
    all_gather x1, blocking collectives, per_device(): lax.all_gather(delta, 'col', axis=1, tiled=True)  50.8 us
    all_gather x1, blocking collectives, per_device(): lax.all_gather(keys, 'row', axis=1, tiled=True)  48 us
    all_gather x1, blocking collectives, per_device(): lax.all_gather(lse, 'col', axis=1, tiled=True)  37.9 us
    add x8, other arithmetic, advance(): return ((key_sum + key_term, value_sum + value_term), query_term)  22.6 us
    squeeze x16, local copies, waits for them, and re-layouts, query_pass(): lax.scan(advance, (empty_sums, empty_sums), block_inputs)  15.6 us
  transfers between devices with their start and end apart: 6, of which 3 were waited for; matrix products, arithmetic and copies ran while one was open for 1% of the time, Pallas kernels for 0%

profile of v1, /device:TPU:8, one launch (start us, length us, event | category | flops | bytes accessed | tf_op | source)
XLA Modules:
  0.0 582.4 jit_solution(5088837384334289093)
XLA Ops:
  8.7 1.7 stack.2
  10.3 11.5 %all-to-all-start = ((bf16[8,1024,32]{1,2,0:T(8,128)(2,1)}), bf16[8,1024,32]{1,2,0:T(8,128)(2,1)S(1)}, u32[]{:S(2)}, u32[]{:S(2)}) async-start(bf16[8,1024,32]{1,2,0:T(8,128)(2,1)} %stack.2), calls=%async_computation | async-start | bytes 1048576 | tf_op jit(solution)/shard_map/all_to_all | solution.py:105
  22.9 48.0 %all_gather.16 = bf16[1024,256]{0,1:T(8,128)(2,1)S(1)} all-gather(bf16[1024,32]{0,1:T(8,128)(2,1)S(1)} %copy-done.1), channel_id=1, replica_groups=mesh['row'=8,'col'=32] {'row'}, dimensions={1}, use_global_device_ids=true | all-gather | bytes 589824 | tf_op jit(solution)/shard_map/all_gather | solution.py:103
  71.3 50.8 %all_gather.19 = f32[2,4096]{0,1:T(8,128)} all-gather(f32[2,128]{0,1:T(8,128)S(1)} %bitcast.59), channel_id=1, replica_groups=mesh['row'=8,'col'=32] {'col'}, dimensions={1}, use_global_device_ids=true | all-gather | bytes 33792 | tf_op jit(solution)/shard_map/all_gather | solution.py:114
  122.1 2.2 copy.19
  124.3 37.9 %all_gather.17 = f32[2,4096]{1,0:T(2,128)S(1)} all-gather(f32[2,128]{1,0:T(2,128)S(1)} %copy-done.2), channel_id=1, replica_groups=mesh['row'=8,'col'=32] {'col'}, dimensions={1}, use_global_device_ids=true | all-gather | bytes 33792 | tf_op jit(solution)/shard_map/all_gather | solution.py:113
  162.5 87.2 %while.15 = (s32[]{:T(128)}, f32[1024,256]{0,1:T(8,128)}, f32[1024,256]{0,1:T(8,128)S(1)}, f32[8,512,256]{2,1,0:T(8,128)}, bf16[8,512,256]{2,1,0:T(8,128)(2,1)},...) while((s32[]{:T(128)}, f32[1024,256]{0,1:T(8,128)}, ...), condition=%wide.region_2.3_spmd.clone, body=%wide.region_1.2_spmd.clone.sunk | while | flops 1352269824 | bytes 34631860 | solution.py:87
  163.6 1.0 dynamic-slice_bitcast_fusion.4
  169.5 1.8 maximum_add_fusion.3
  173.4 1.0 dynamic-slice_bitcast_fusion.4
  179.3 3.0 maximum_add_fusion.3
  184.4 1.0 dynamic-slice_bitcast_fusion.4
  190.4 3.0 maximum_add_fusion.3
  201.4 3.0 maximum_add_fusion.3
  212.5 3.0 maximum_add_fusion.3
  223.5 3.0 maximum_add_fusion.3
  234.6 3.0 maximum_add_fusion.3
  245.6 3.0 maximum_add_fusion.3
  251.8 86.0 %reduce-scatter.8.cloned.1.call-done = f32[1024,32]{0,1:T(8,128)} async-done(((f32[1024,256]{0,1:T(8,128)}), f32[1024,32]{0,1:T(8,128)}) %reduce-scatter.8.cloned.1.call-update) | async-done | bytes 131088 | tf_op jit(solution)/shard_map/reduce_scatter | solution.py:122
  337.9 1.5 convert_element_type.31
  339.4 85.6 %reduce-scatter.6.cloned.1.call-done = f32[1024,32]{0,1:T(8,128)} async-done(((f32[1024,256]{0,1:T(8,128)}), f32[1024,32]{0,1:T(8,128)}) %reduce-scatter.6.cloned.1.call-update) | async-done | bytes 131088 | tf_op jit(solution)/shard_map/reduce_scatter | solution.py:121
  425.0 1.5 multiply_convert_fusion.2
  426.5 147.8 %reduce-scatter.4.cloned.1.call-done = f32[128,256]{1,0:T(8,128)} async-done(((f32[4096,256]{1,0:T(8,128)}), f32[128,256]{1,0:T(8,128)}) %reduce-scatter.4.cloned.1.call-update) | async-done | bytes 131088 | tf_op jit(solution)/shard_map/reduce_scatter | solution.py:119
  574.4 1.5 multiply_convert_fusion.3
  (160 shorter events, 66.0 us)
Async XLA Ops:
  7.2 15.7 %copy-start.1 = (bf16[1024,32]{0,1:T(8,128)(2,1)S(1)}, bf16[1024,32]{0,1:T(8,128)(2,1)}, u32[]{:S(2)}) copy-start(bf16[1024,32]{0,1:T(8,128)(2,1)} %param.9) | copy-start | bytes 196612
  7.2 155.3 %all-gather.3.cloned.1.call-start = ((), (), s32[]{:S(2)}) async-start(), calls=%async_computation.4 | async-start | bytes 2162688 | tf_op jit(solution)/shard_map/all_gather | solution.py:109
  7.9 154.6 %all-gather.5.cloned.1.call-start = ((), (), s32[]{:S(2)}) async-start(), calls=%async_computation.5 | async-start | bytes 2162688 | tf_op jit(solution)/shard_map/all_gather | solution.py:110
  10.3 151.9 %all-to-all-start = ((bf16[8,1024,32]{1,2,0:T(8,128)(2,1)}), bf16[8,1024,32]{1,2,0:T(8,128)(2,1)S(1)}, u32[]{:S(2)}, u32[]{:S(2)}) async-start(bf16[8,1024,32]{1,2,0:T(8,128)(2,1)} %stack.2), calls=%async_computation | async-start | bytes 1048576 | tf_op jit(solution)/shard_map/all_to_all | solution.py:105
  21.9 316.0 %reduce-scatter.8.cloned.1.call-start = ((), (), s32[]{:S(2)}) async-start(), calls=%async_computation.8 | async-start | bytes 1179648 | tf_op jit(solution)/shard_map/reduce_scatter | solution.py:122
  71.3 53.0 %copy-start.2 = (f32[2,128]{1,0:T(2,128)S(1)}, f32[2,128]{1,0:T(2,128)}, u32[]{:S(2)}) copy-start(f32[2,128]{1,0:T(2,128)} %param.13) | copy-start | bytes 3076
  249.7 1.0 copy-start
  250.7 174.3 %reduce-scatter.6.cloned.1.call-start = ((), (), s32[]{:S(2)}) async-start(), calls=%async_computation.7 | async-start | bytes 1179648 | tf_op jit(solution)/shard_map/reduce_scatter | solution.py:121
  251.2 323.1 %reduce-scatter.4.cloned.1.call-start = ((), (), s32[]{:S(2)}) async-start(), calls=%async_computation.6 | async-start | bytes 4325376 | tf_op jit(solution)/shard_map/reduce_scatter | solution.py:119
Sparse Core Ops, SparseCore 0:
  9.9 67.4 all-gather.2
  79.2 64.2 all-gather.4
  250.8 87.0 reduce-scatter.7
  342.2 82.7 reduce-scatter.5
  427.4 146.9 reduce-scatter.3
